TPU v7x, 32 devices: a whole 2x2x4 slice. The times are simulated.
32 devices in a mesh: real: 4 (over z), rows: 4 (over y, core), field: 2 (over x).
Axes of the slice: x: 2, y: 2, z: 4, core: 2. Of those that a mesh axis runs over, the one named last changes fastest.
Arguments:
- sims: bfloat16 [4, 2, 2048, 2048], P('real', 'field', 'rows'), may hold values from -6 to 6
- data: bfloat16 [2, 2048, 2048], P('field', 'rows'), may hold values from -6 to 6
- mask_flags: int32 [16, 16], P('rows'), may hold values 0 or 1
- bins: int32 [512, 512], P(None, 'rows'), may hold values from 0 to 63
- cl_signal: float32 [2, 64], P('field'), may hold values from 0.5 to 4
- cl_noise: float32 [2, 64], P('field'), may hold values from 0.1 to 2
- norm: float32 [64], replicated, may hold values from 0.5 to 2
- matching: int32 [4], replicated, may hold values from 0 to 3, each once
Outputs:
- estimates: float32 [4, 2, 2, 512, 512], P('real', None, None, None, 'rows')
Inputs may be any that keep to these rules, and one draw needn't show every extreme that they name: `matching`: each realization index appears exactly once.
All inputs are finite; a program needn't handle non-finite values. No bound on the sum of `mask_flags` on one device may be relied on, other than what follows from the above.
Results may differ from a plain program's by a relative error of at most 0.011.
Values may be sent and summed in bfloat16 or wider, within the bound.
A program may use at most 128 MiB of HBM per device.

v0:
```python
import math
import jax
import jax.numpy as jnp
from jax import lax
from jax.sharding import PartitionSpec as P

TILE = 128


def tables(npix, kf, scale):
    pixel = jnp.arange(npix, dtype=jnp.int32)
    freq = jnp.arange(kf, dtype=jnp.int32) - kf // 2
    phase = jnp.mod(pixel[:, None] * freq[None, :], npix)
    angle = phase.astype(jnp.float32) * (2.0 * math.pi / npix)
    return (
        (jnp.cos(angle) * scale).astype(jnp.bfloat16),
        (jnp.sin(angle) * scale).astype(jnp.bfloat16),
    )


def expand_mask(flags, tile):
    first, second = flags.shape
    full = jnp.broadcast_to(flags[:, None, :, None], (first, tile, second, tile))
    return full.reshape(first * tile, second * tile) > 0


def column_part(maps, cos_t, sin_t):
    count, height, width = maps.shape
    flat = maps.reshape(count * height, width)
    a_re = (
        jnp.dot(flat, cos_t, preferred_element_type=jnp.float32)
        .astype(jnp.bfloat16)
        .reshape(count, height, -1)
    )
    a_im = (
        (-jnp.dot(flat, sin_t, preferred_element_type=jnp.float32))
        .astype(jnp.bfloat16)
        .reshape(count, height, -1)
    )
    return (a_re, a_im)


def row_part(a_re, a_im, cos_t, sin_t):
    a_re, a_im = (
        lax.all_to_all(a_re, "rows", split_axis=2, concat_axis=1, tiled=True),
        lax.all_to_all(a_im, "rows", split_axis=2, concat_axis=1, tiled=True),
    )
    x_re = jnp.einsum("yk,myj->mkj", cos_t, a_re, preferred_element_type=jnp.float32) + jnp.einsum(
        "yk,myj->mkj", sin_t, a_im, preferred_element_type=jnp.float32
    )
    x_im = jnp.einsum("yk,myj->mkj", cos_t, a_im, preferred_element_type=jnp.float32) - jnp.einsum(
        "yk,myj->mkj", sin_t, a_re, preferred_element_type=jnp.float32
    )
    return (x_re, x_im)


def inverse(z_re, z_im, icos, isin):
    count = z_re.shape[0]
    y_re = (
        jnp.einsum("yk,mkj->myj", icos, z_re, preferred_element_type=jnp.float32)
        - jnp.einsum("yk,mkj->myj", isin, z_im, preferred_element_type=jnp.float32)
    ).astype(jnp.bfloat16)
    y_im = (
        jnp.einsum("yk,mkj->myj", icos, z_im, preferred_element_type=jnp.float32)
        + jnp.einsum("yk,mkj->myj", isin, z_re, preferred_element_type=jnp.float32)
    ).astype(jnp.bfloat16)
    y_re, y_im = (
        lax.all_to_all(y_re, "rows", split_axis=1, concat_axis=2, tiled=True),
        lax.all_to_all(y_im, "rows", split_axis=1, concat_axis=2, tiled=True),
    )
    height = y_re.shape[1]
    flat_re = y_re.reshape(count * height, -1)
    flat_im = y_im.reshape(count * height, -1)
    out = jnp.dot(flat_re, icos.T, preferred_element_type=jnp.float32) - jnp.dot(
        flat_im, isin.T, preferred_element_type=jnp.float32
    )
    return out.astype(jnp.bfloat16).reshape(count, height, -1)


def filter_legs(x_re, x_im, wcell, gcell, lx, ly):
    grad_x = lx * gcell
    grad_y = ly * gcell
    z_re = jnp.stack([wcell * x_re, -grad_x * x_im, -grad_y * x_im])
    z_im = jnp.stack([wcell * x_im, grad_x * x_re, grad_y * x_re])
    return (z_re.astype(jnp.bfloat16), z_im.astype(jnp.bfloat16))


def select_rows(piece, partner_id):
    count = piece.shape[0]
    hit = jnp.arange(count, dtype=jnp.int32) == partner_id
    hit = hit.reshape((count,) + (1,) * (piece.ndim - 1))
    return jnp.sum(jnp.where(hit, piece, jnp.zeros_like(piece)), axis=0).astype(piece.dtype)


def lookup_cells(bins, values):
    nbins = values.shape[0]
    match_bin = bins[:, :, None] == jnp.arange(nbins, dtype=jnp.int32)[None, None, :]
    return jnp.sum(jnp.where(match_bin, values[None, None, :], jnp.zeros((), jnp.float32)), axis=2)


def body(sims, data, mask_flags, bins, cl_signal, cl_noise, norm, matching):
    npix = sims.shape[3]
    kf = bins.shape[0]
    cols = bins.shape[1]
    mask = expand_mask(mask_flags, TILE)
    stacked = jnp.concatenate([sims[0], data], axis=0)
    masked = jnp.where(mask[None], stacked, jnp.zeros_like(stacked))
    cos_t, sin_t = tables(npix, kf, npix ** (-0.5))
    icos, isin = tables(npix, kf, kf ** (-0.5))
    step_size = 2.0 * math.pi / npix
    col_freq = (lax.axis_index("rows") * cols + jnp.arange(cols, dtype=jnp.int32) - kf // 2).astype(
        jnp.float32
    ) * step_size
    row_freq = (jnp.arange(kf, dtype=jnp.int32) - kf // 2).astype(jnp.float32) * step_size
    lx = jnp.broadcast_to(col_freq[None, :], (kf, cols))
    ly = jnp.broadcast_to(row_freq[:, None], (kf, cols))
    weight_vals = 1.0 / (cl_signal[0] + cl_noise[0])
    grad_vals = cl_signal[0] * weight_vals
    wcell = lookup_cells(bins, weight_vals)
    gcell = lookup_cells(bins, grad_vals)
    ncell = lookup_cells(bins, norm)
    first_re, first_im = column_part(masked, cos_t, sin_t)
    x_re, x_im = row_part(first_re, first_im, cos_t, sin_t)
    own_re, own_im = filter_legs(x_re[0], x_im[0], wcell, gcell, lx, ly)
    dat_re, dat_im = filter_legs(x_re[1], x_im[1], wcell, gcell, lx, ly)
    legs = inverse(
        jnp.concatenate([own_re, dat_re], axis=0),
        jnp.concatenate([own_im, dat_im], axis=0),
        icos,
        isin,
    )
    sim_legs = legs[0:3]
    data_legs = legs[3:6].astype(jnp.float32)
    real_index = lax.axis_index("real")
    partner_id = jnp.sum(
        jnp.where(jnp.arange(matching.shape[0], dtype=jnp.int32) == real_index, matching, 0)
    )
    empty = jnp.zeros_like(x_re[0])
    p_re = empty + select_rows(
        lax.all_gather(x_re[0:1].astype(jnp.bfloat16), "real", axis=0, tiled=True).astype(
            jnp.float32
        ),
        partner_id,
    )
    p_im = empty + select_rows(
        lax.all_gather(x_im[0:1].astype(jnp.bfloat16), "real", axis=0, tiled=True).astype(
            jnp.float32
        ),
        partner_id,
    )
    z_re, z_im = filter_legs(p_re, p_im, wcell, gcell, lx, ly)
    partner_legs = inverse(z_re, z_im, icos, isin)
    own = sim_legs.astype(jnp.float32)
    other = partner_legs.astype(jnp.float32)
    ds_x = data_legs[1] * own[0] + own[1] * data_legs[0]
    ss_x = own[1] * other[0] + other[1] * own[0]
    ds_y = data_legs[2] * own[0] + own[2] * data_legs[0]
    ss_y = own[2] * other[0] + other[2] * own[0]
    products = jnp.stack([ds_x, ss_x, ds_y, ss_y]).astype(jnp.bfloat16)
    height = products.shape[1]
    mine = lax.all_to_all(products[None], "field", split_axis=1, concat_axis=0, tiled=True)
    sources = mine.shape[0]
    part_re, part_im = column_part(mine.reshape(sources * 2, height, npix), cos_t, sin_t)
    sum_re = jnp.sum(part_re.astype(jnp.float32).reshape(sources, 2, height, -1), axis=0)
    sum_im = jnp.sum(part_im.astype(jnp.float32).reshape(sources, 2, height, -1), axis=0)
    s_re, s_im = row_part(sum_re.astype(jnp.bfloat16), sum_im.astype(jnp.bfloat16), cos_t, sin_t)
    direction = jnp.where(lax.axis_index("field") == 0, lx, ly)
    scale = ncell * direction
    terms = jnp.stack([-scale * s_im, scale * s_re], axis=1)
    total = lax.psum(terms.astype(jnp.bfloat16), "field").astype(jnp.float32)
    return total[None]


def solution(mesh):
    in_specs = (
        P("real", "field", "rows", None),
        P("field", "rows", None),
        P("rows", None),
        P(None, "rows"),
        P("field", None),
        P("field", None),
        P(),
        P(),
    )
    out_specs = P("real", None, None, None, "rows")
    return jax.shard_map(body, mesh=mesh, in_specs=in_specs, out_specs=out_specs, check_vma=False)
```

profile of v0, /device:TPU:0, one launch (start us, length us, event | category | flops | bytes accessed | tf_op | source)
XLA Modules:
  0.0 774.8 jit_solution(14107730076439929142)
XLA Ops:
  10.6 16.8 %negate_convert_fusion.1 = bf16[1024,512]{1,0:T(8,128)(2,1)S(1)} fusion(bf16[1024,2048]{1,0:T(8,128)(2,1)S(1)} %bitcast.283, s32[512]{0:T(512)S(1)} %iota_add_fusion), kind=kOutput, calls=%fused_computation.84 | convolution fusion | flops 2165309440 | bytes 5244928 | tf_op jit(solution)/shard_map/dot_general | solution.py:36
  29.5 4.4 all-to-all-start.1
  34.0 18.9 %fusion.65 = bf16[1024,512]{1,0:T(8,128)(2,1)S(1)} fusion(bf16[1024,2048]{1,0:T(8,128)(2,1)} %bitcast.284, s32[512]{0:T(512)S(1)} %iota_add_fusion), kind=kOutput, calls=%fused_computation.94 | convolution fusion | flops 2164785152 | bytes 5244928 | tf_op jit(solution)/shard_map/dot_general | solution.py:31
  55.7 16.3 %select_reduce_fusion.2 = (f32[512,128]{1,0:T(8,128)}, f32[512,128]{1,0:T(8,128)S(1)}, f32[512,128]{1,0:T(8,128)S(1)}) fusion(f32[64]{0:T(128)S(1)} %copy-done.12, s32[512,128]{1,0:T(8,128)S(1)} %copy-done.7, f32[64]{0:T(128)S(1)} %get-tuple-element.12, f32[64]{0:T(128)S(1)} %get-tuple-element.13), kind=kLoop, calls=%fused_computation.3 | loop fusion | flops 29163520 | bytes 1049344 | tf_op jit(solution)/shard_map/reduce_sum | solution.py:98
  72.0 3.7 all-to-all-start
  80.3 16.7 %fusion.46 = f32[2,128,512]{2,1,0:T(8,128)} fusion(bf16[2,2048,128]{1,2,0:T(8,128)(2,1)S(1)} %all_to_all.110, s32[512]{0:T(512)S(1)} %iota_add_fusion), kind=kOutput, calls=%fused_computation.74 | convolution fusion | flops 553648128 | bytes 1574912 | tf_op jit(solution)/shard_map/yk,myj->mkj/dot_general | solution.py:48
  99.6 16.5 %fusion.44 = f32[2,128,512]{2,1,0:T(8,128)S(1)} fusion(bf16[2,2048,128]{1,2,0:T(8,128)(2,1)S(1)} %all_to_all.106, s32[512]{0:T(512)S(1)} %iota_add_fusion), kind=kOutput, calls=%fused_computation.72 | convolution fusion | flops 553648128 | bytes 1574912 | tf_op jit(solution)/shard_map/yk,myj->mkj/dot_general | solution.py:51
  116.1 17.2 %fusion.69 = f32[2,512,128]{1,2,0:T(8,128)S(1)} fusion(f32[2,128,512]{2,1,0:T(8,128)S(1)} %copy-done.16, bf16[2,2048,128]{1,2,0:T(8,128)(2,1)} %copy-done.6, s32[512]{0:T(512)S(1)} %iota_add_fusion), kind=kOutput, calls=%fused_computation.96 | convolution fusion | flops 553779200 | bytes 2099200 | tf_op jit(solution)/shard_map/yk,myj->mkj/dot_general | solution.py:48
  133.4 15.9 %fusion.75 = f32[2,512,128]{1,2,0:T(8,128)S(1)} fusion(f32[2,128,512]{2,1,0:T(8,128)S(1)} %fusion.44, bf16[2,2048,128]{1,2,0:T(8,128)(2,1)S(1)} %copy-done.5, s32[512]{0:T(512)S(1)} %iota_add_fusion), kind=kOutput, calls=%fused_computation.98 | convolution fusion | flops 553779200 | bytes 2099200 | tf_op jit(solution)/shard_map/yk,myj->mkj/dot_general | solution.py:51
  151.5 17.2 %all_gather.6 = bf16[4,512,128]{2,1,0:T(8,128)(2,1)S(1)} all-gather(bf16[1,512,128]{2,1,0:T(8,128)(2,1)S(1)} %copy.78), channel_id=1, replica_groups=mesh['real'=4,'rows'=4,'field'=2] {'real'}, dimensions={0}, use_global_device_ids=true | all-gather | bytes 655360 | tf_op jit(solution)/shard_map/all_gather | solution.py:140
  168.8 15.6 %all_gather.7 = bf16[4,512,128]{2,1,0:T(8,128)(2,1)S(1)} all-gather(bf16[1,512,128]{2,1,0:T(8,128)(2,1)S(1)} %copy.80), channel_id=1, replica_groups=mesh['real'=4,'rows'=4,'field'=2] {'real'}, dimensions={0}, use_global_device_ids=true | all-gather | bytes 655360 | tf_op jit(solution)/shard_map/all_gather | solution.py:146
  185.2 16.0 %fusion.34 = f32[3,128,2048]{2,1,0:T(8,128)S(1)} fusion(s32[512]{0:T(512)S(1)} %iota_add_fusion, bf16[1,512,128]{1,2,0:T(8,128)(2,1)S(1)} %get-tuple-element.25, bf16[1,512,128]{1,2,0:T(8,128)(2,1)S(1)} %get-tuple-element.24, bf16[1,512,128]{1,2,0:T(8,128)(2,1)S(1)} %get-tuple-element.36), kind=kOutput, calls=%fused_computation.62 | convolution fusion | flops 822476800 | bytes 3540992 | tf_op jit(solution)/shard_map/yk,mkj->myj/dot_general | solution.py:60
  201.2 17.3 %fusion.32 = f32[3,128,2048]{2,1,0:T(8,128)} fusion(s32[512]{0:T(512)S(1)} %iota_add_fusion, bf16[1,512,128]{1,2,0:T(8,128)(2,1)S(1)} %get-tuple-element.34, bf16[1,512,128]{1,2,0:T(8,128)(2,1)S(1)} %get-tuple-element.35, bf16[1,512,128]{1,2,0:T(8,128)(2,1)S(1)} %get-tuple-element.37), kind=kOutput, calls=%fused_computation.60 | convolution fusion | flops 822476800 | bytes 3540992 | tf_op jit(solution)/shard_map/yk,mkj->myj/dot_general | solution.py:64
  218.5 16.7 %fusion.22 = bf16[3,2048,128]{1,2,0:T(8,128)(2,1)S(1)} fusion(f32[3,128,2048]{2,1,0:T(8,128)S(1)} %fusion.34, s32[512]{0:T(512)S(1)} %iota_add_fusion, bf16[1,512,128]{1,2,0:T(8,128)(2,1)S(1)} %get-tuple-element.34, bf16[1,512,128]{1,2,0:T(8,128)(2,1)S(1)} %get-tuple-element.35, bf16[1,512,128]{1,2,0:T(8,128)(2,1)S(1)} %get-tuple-element.37), kind=kOutput, calls=%fused_computation.50 | convolution fusion | flops 824049664 | bytes 5113856 | tf_op jit(solution)/shard_map/yk,mkj->myj/dot_general | solution.py:61
  235.2 2.6 copy.82
  237.8 3.8 all-to-all-start.4
  241.6 18.6 %fusion.23 = bf16[3,2048,128]{1,2,0:T(8,128)(2,1)} fusion(f32[3,128,2048]{2,1,0:T(8,128)} %fusion.32, s32[512]{0:T(512)S(1)} %iota_add_fusion, bf16[1,512,128]{1,2,0:T(8,128)(2,1)S(1)} %get-tuple-element.25, bf16[1,512,128]{1,2,0:T(8,128)(2,1)S(1)} %get-tuple-element.24, bf16[1,512,128]{1,2,0:T(8,128)(2,1)S(1)} %get-tuple-element.36), kind=kOutput, calls=%fused_computation.51 | convolution fusion | flops 824049664 | bytes 5113856 | tf_op jit(solution)/shard_map/yk,mkj->myj/dot_general | solution.py:65
  260.1 4.2 copy.84
  267.7 20.1 %fusion.38 = f32[6,128,2048]{2,1,0:T(8,128)} fusion(bf16[6,512,128]{1,2,0:T(8,128)(2,1)} %get-tuple-element.33, s32[512]{0:T(512)S(1)} %iota_add_fusion), kind=kOutput, calls=%fused_computation.66 | convolution fusion | flops 1627389952 | bytes 7079936 | tf_op jit(solution)/shard_map/yk,mkj->myj/dot_general | solution.py:60
  287.9 4.5 all-to-all-start.5
  293.8 20.4 %fusion.20 = bf16[6,2048,128]{1,2,0:T(8,128)(2,1)} fusion(f32[6,128,2048]{2,1,0:T(8,128)} %fusion.38, bf16[6,512,128]{1,2,0:T(8,128)(2,1)} %fusion.125, s32[512]{0:T(512)S(1)} %iota_add_fusion), kind=kOutput, calls=%fused_computation.47 | convolution fusion | flops 1630535680 | bytes 10225664 | tf_op jit(solution)/shard_map/yk,mkj->myj/dot_general | solution.py:61
  314.2 6.3 copy.74
  320.6 5.2 all-to-all-start.2
  325.8 16.4 %fusion.36 = f32[6,128,2048]{2,1,0:T(8,128)S(1)} fusion(bf16[6,512,128]{1,2,0:T(8,128)(2,1)S(1)} %copy-done.9, s32[512]{0:T(512)S(1)} %iota_add_fusion), kind=kOutput, calls=%fused_computation.64 | convolution fusion | flops 1627389952 | bytes 7079936 | tf_op jit(solution)/shard_map/yk,mkj->myj/dot_general | solution.py:64
  342.3 22.0 %fusion.21 = bf16[6,2048,128]{1,2,0:T(8,128)(2,1)} fusion(f32[6,128,2048]{2,1,0:T(8,128)S(1)} %fusion.36, bf16[6,512,128]{1,2,0:T(8,128)(2,1)S(1)} %copy-done.11, s32[512]{0:T(512)S(1)} %iota_add_fusion), kind=kOutput, calls=%fused_computation.48 | convolution fusion | flops 1630535680 | bytes 10225664 | tf_op jit(solution)/shard_map/yk,mkj->myj/dot_general | solution.py:65
  364.2 6.3 copy.76
  372.1 3.1 copy.85
  375.2 20.1 %fusion.60 = f32[1536,2048]{1,0:T(8,128)} fusion(s32[512]{0:T(512)S(1)} %iota_add_fusion, bf16[192,8,4,128]{3,2,1,0:T(4,128)(2,1)S(1)} %bitcast.298), kind=kOutput, calls=%fused_computation.89 | convolution fusion | flops 3238002688 | bytes 14157824 | tf_op jit(solution)/shard_map/dot_general | solution.py:74
  395.3 4.8 all-to-all-start.3
  400.2 22.3 %fusion = f32[1536,2048]{1,0:T(8,128)} fusion(f32[1536,2048]{1,0:T(8,128)} %fusion.60, s32[512]{0:T(512)S(1)} %iota_add_fusion, bf16[192,8,4,128]{3,2,1,0:T(4,128)(2,1)S(1)} %bitcast.297), kind=kOutput, calls=%fused_computation.7 | convolution fusion | flops 3247439872 | bytes 26740736 | tf_op jit(solution)/shard_map/dot_general | solution.py:74
  422.4 4.6 copy.75
  427.0 23.9 %fusion.17 = f32[3072,2048]{1,0:T(8,128)} fusion(bf16[384,8,4,128]{3,2,1,0:T(4,128)(2,1)S(1)} %bitcast.293, s32[512]{0:T(512)S(1)} %iota_add_fusion), kind=kOutput, calls=%fused_computation.42 | convolution fusion | flops 6459228160 | bytes 28313600 | tf_op jit(solution)/shard_map/dot_general | solution.py:74
  450.9 4.6 copy.77
  455.5 24.4 %subtract_convert_fusion = bf16[3072,2048]{1,0:T(8,128)(2,1)S(1)} fusion(f32[3072,2048]{1,0:T(8,128)} %fusion.17, bf16[384,8,4,128]{3,2,1,0:T(4,128)(2,1)S(1)} %bitcast.292, s32[512]{0:T(512)S(1)} %iota_add_fusion), kind=kOutput, calls=%fused_computation | convolution fusion | flops 6471811072 | bytes 40896512 | tf_op jit(solution)/shard_map/dot_general | solution.py:74
  479.9 9.4 %slice_convert_fusion.1 = (f32[1536,2048]{1,0:T(8,128)}, f32[1536,2048]{1,0:T(8,128)}) fusion(bf16[3072,2048]{1,0:T(8,128)(2,1)S(1)} %subtract_convert_fusion), kind=kLoop, calls=%fused_computation.9 | loop fusion | flops 6291456 | bytes 37748736 | tf_op jit(solution)/shard_map/convert_element_type | solution.py:133
  489.3 15.6 %fusion.24 = (bf16[1,1,512,2048]{3,2,1,0:T(8,128)(2,1)S(1)}, bf16[1,1,512,2048]{3,2,1,0:T(8,128)(2,1)S(1)}, bf16[1,1,512,2048]{3,2,1,0:T(8,128)(2,1)S(1)}, bf16[1,1,512,2048]{3,2,1,0:T(8,128)(2,1)}) fusion(f32[1536,2048]{1,0:T(8,128)} %get-tuple-element.20, f32[1536,2048]{1,0:T(8,128)} %get-tuple-element.21, f32[1536,2048]{1,0:T(8,128)} %fusion), kind=kLoop, calls=%fused_computation.52 | loop fusion | flops 16777216 | bytes 46137344 | tf_op jit(solution)/shard_map/stack | solution.py:159
  504.9 5.7 maximum_bitcast_fusion
  510.6 6.9 all-to-all-start.6
  517.6 93.2 %all-to-all-done.6 = bf16[1,4,512,2048]{3,2,0,1:T(8,128)(2,1)} async-done(((bf16[1,4,512,2048]{3,2,0,1:T(8,128)(2,1)}), bf16[1,4,512,2048]{3,2,0,1:T(8,128)(2,1)}, u32[]{:S(2)}, u32[]{:S(2)}) %all-to-all-start.6) | async-done | bytes 8388640 | tf_op jit(solution)/shard_map/all_to_all | solution.py:161
  610.8 21.3 %negate_convert_fusion = bf16[2048,512]{1,0:T(8,128)(2,1)S(1)} fusion(bf16[2048,2048]{1,0:T(8,128)(2,1)} %bitcast.37, s32[512]{0:T(512)S(1)} %iota_add_fusion), kind=kOutput, calls=%fused_computation.31 | convolution fusion | flops 4313841664 | bytes 10487808 | tf_op jit(solution)/shard_map/dot_general | solution.py:36
  635.4 3.7 all-to-all-start.7
  639.1 22.1 %convolution_convert_fusion = bf16[2048,512]{1,0:T(8,128)(2,1)} fusion(bf16[2048,2048]{1,0:T(8,128)(2,1)} %bitcast.37, s32[512]{0:T(512)S(1)} %iota_add_fusion), kind=kOutput, calls=%fused_computation.49 | convolution fusion | flops 4312793088 | bytes 10487808 | tf_op jit(solution)/shard_map/dot_general | solution.py:31
  665.7 3.5 all-to-all-start.8
  670.0 16.3 %fusion.40 = f32[2,128,512]{2,1,0:T(8,128)S(1)} fusion(bf16[2,2048,128]{1,2,0:T(8,128)(2,1)S(1)} %bitcast.299, s32[512]{0:T(512)S(1)} %iota_add_fusion), kind=kOutput, calls=%fused_computation.68 | convolution fusion | flops 553648128 | bytes 1574912 | tf_op jit(solution)/shard_map/yk,myj->mkj/dot_general | solution.py:48
  686.6 16.1 %fusion.42 = f32[2,128,512]{2,1,0:T(8,128)S(1)} fusion(bf16[2,2048,128]{1,2,0:T(8,128)(2,1)S(1)} %bitcast.301, s32[512]{0:T(512)S(1)} %iota_add_fusion), kind=kOutput, calls=%fused_computation.70 | convolution fusion | flops 553648128 | bytes 1574912 | tf_op jit(solution)/shard_map/yk,myj->mkj/dot_general | solution.py:51
  702.8 16.1 %fusion.102 = bf16[2,1,512,128]{2,3,0,1:T(8,128)(2,1)S(1)} fusion(f32[2,128,512]{2,1,0:T(8,128)S(1)} %fusion.40, bf16[2,2048,128]{1,2,0:T(8,128)(2,1)S(1)} %bitcast.302, s32[512]{0:T(512)S(1)} %iota_add_fusion, f32[512,128]{0,1:T(8,128)S(1)} %copy.93), kind=kOutput, calls=%fused_computation.107 | convolution fusion | flops 554041344 | bytes 2099200 | tf_op jit(solution)/shard_map/yk,myj->mkj/dot_general | solution.py:48
  718.8 16.1 %fusion.105 = bf16[2,1,512,128]{2,3,0,1:T(8,128)(2,1)S(1)} fusion(f32[2,128,512]{2,1,0:T(8,128)S(1)} %fusion.42, bf16[2,2048,128]{1,2,0:T(8,128)(2,1)S(1)} %bitcast.300, s32[512]{0:T(512)S(1)} %iota_add_fusion, f32[512,128]{0,1:T(8,128)S(1)} %copy.67), kind=kOutput, calls=%fused_computation.108 | convolution fusion | flops 554041344 | bytes 2099200 | tf_op jit(solution)/shard_map/yk,myj->mkj/dot_general | solution.py:51
  735.8 29.7 %all-reduce.2.cloned.1.call-done = bf16[1,2,2,512,128]{3,4,1,2,0:T(8,128)(2,1)} async-done(((bf16[1,2,2,512,128]{3,4,1,2,0:T(8,128)(2,1)}), bf16[1,2,2,512,128]{3,4,1,2,0:T(8,128)(2,1)}) %all-reduce.2.cloned.1.call-update) | async-done | bytes 524304 | tf_op jit(solution)/shard_map/psum | solution.py:170
  (90 shorter events, 37.3 us)
Async XLA Ops:
  6.5 1.8 copy-start.2
  10.6 16.8 %copy-start = (bf16[2,512,2048]{2,1,0:T(8,128)(2,1)}, bf16[2,512,2048]{2,1,0:T(8,128)(2,1)S(1)}, u32[]{:S(2)}) copy-start(bf16[2,512,2048]{2,1,0:T(8,128)(2,1)S(1)} %maximum_select_fusion) | copy-start | bytes 12582916
  29.5 42.5 %all-to-all-start.1 = ((bf16[2,512,512]{1,0,2:T(2,128)(2,1)}), bf16[2,512,512]{1,0,2:T(2,128)(2,1)S(1)}, u32[]{:S(2)}, u32[]{:S(2)}) async-start(bf16[2,512,512]{1,0,2:T(2,128)(2,1)} %copy.71), calls=%async_computation.1 | async-start | bytes 2097152 | tf_op jit(solution)/shard_map/all_to_all | solution.py:46
  33.9 21.0 %copy-start.13 = (f32[1,64]{1,0:T(1,128)S(1)}, f32[1,64]{1,0:T(1,128)}, u32[]{:S(2)}) copy-start(f32[1,64]{1,0:T(1,128)} %param.12) | copy-start | bytes 772
  33.9 21.0 %copy-start.14 = (f32[1,64]{1,0:T(1,128)S(1)}, f32[1,64]{1,0:T(1,128)}, u32[]{:S(2)}) copy-start(f32[1,64]{1,0:T(1,128)} %param.13) | copy-start | bytes 772
  34.0 21.0 %copy-start.15 = (s32[4]{0:T(128)S(1)}, s32[4]{0:T(128)}, u32[]{:S(2)}) copy-start(s32[4]{0:T(128)} %param.15) | copy-start | bytes 52
  34.0 21.7 %copy-start.7 = (s32[512,128]{1,0:T(8,128)S(1)}, s32[512,128]{1,0:T(8,128)}, u32[]{:S(2)}) copy-start(s32[512,128]{1,0:T(8,128)} %param.11) | copy-start | bytes 786436
  34.0 21.7 %copy-start.12 = (f32[64]{0:T(128)S(1)}, f32[64]{0:T(128)}, u32[]{:S(2)}) copy-start(f32[64]{0:T(128)} %param.14) | copy-start | bytes 772
  72.0 25.0 %all-to-all-start = ((bf16[2,512,512]{1,0,2:T(2,128)(2,1)}), bf16[2,512,512]{1,0,2:T(2,128)(2,1)S(1)}, u32[]{:S(2)}, u32[]{:S(2)}) async-start(bf16[2,512,512]{1,0,2:T(2,128)(2,1)} %copy.69), calls=%async_computation | async-start | bytes 2097152 | tf_op jit(solution)/shard_map/all_to_all | solution.py:45
  80.3 16.7 %copy-start.4 = (bf16[2,2048,128]{1,2,0:T(8,128)(2,1)}, bf16[2,2048,128]{1,2,0:T(8,128)(2,1)S(1)}, u32[]{:S(2)}) copy-start(bf16[2,2048,128]{1,2,0:T(8,128)(2,1)S(1)} %all_to_all.110) | copy-start | bytes 3145732
  98.6 1.0 copy-start.6
  99.6 16.5 %copy-start.16 = (f32[2,128,512]{2,1,0:T(8,128)S(1)}, f32[2,128,512]{2,1,0:T(8,128)}, u32[]{:S(2)}) copy-start(f32[2,128,512]{2,1,0:T(8,128)} %fusion.46) | copy-start | bytes 1572868
  116.1 17.3 %copy-start.5 = (bf16[2,2048,128]{1,2,0:T(8,128)(2,1)S(1)}, bf16[2,2048,128]{1,2,0:T(8,128)(2,1)}, u32[]{:S(2)}) copy-start(bf16[2,2048,128]{1,2,0:T(8,128)(2,1)} %copy-done.4) | copy-start | bytes 3145732
  149.2 35.8 %copy-start.1 = (f32[2,512,128]{1,2,0:T(8,128)}, f32[2,512,128]{1,2,0:T(8,128)S(1)}, u32[]{:S(2)}) copy-start(f32[2,512,128]{1,2,0:T(8,128)S(1)} %fusion.75) | copy-start | bytes 1572868
  149.6 0.9 copy-start.8
  150.5 0.9 copy-start.10
  237.8 50.1 %all-to-all-start.4 = ((bf16[3,2048,128]{2,0,1:T(4,128)(2,1)}), bf16[3,2048,128]{2,0,1:T(4,128)(2,1)S(1)}, u32[]{:S(2)}, u32[]{:S(2)}) async-start(bf16[3,2048,128]{2,0,1:T(4,128)(2,1)} %copy.82), calls=%async_computation.4 | async-start | bytes 4194304 | tf_op jit(solution)/shard_map/all_to_all | solution.py:68
  287.9 32.7 %all-to-all-start.5 = ((bf16[3,2048,128]{2,0,1:T(4,128)(2,1)}), bf16[3,2048,128]{2,0,1:T(4,128)(2,1)}, u32[]{:S(2)}, u32[]{:S(2)}) async-start(bf16[3,2048,128]{2,0,1:T(4,128)(2,1)} %copy.84), calls=%async_computation.5 | async-start | bytes 4194304 | tf_op jit(solution)/shard_map/all_to_all | solution.py:69
  320.6 5.2 copy-start.9
  320.6 74.7 %all-to-all-start.2 = ((bf16[6,2048,128]{2,0,1:T(8,128)(2,1)}), bf16[6,2048,128]{2,0,1:T(8,128)(2,1)}, u32[]{:S(2)}, u32[]{:S(2)}) async-start(bf16[6,2048,128]{2,0,1:T(8,128)(2,1)} %copy.74), calls=%async_computation.2 | async-start | bytes 8388608 | tf_op jit(solution)/shard_map/all_to_all | solution.py:68
  325.8 16.4 %copy-start.11 = (bf16[6,512,128]{1,2,0:T(8,128)(2,1)S(1)}, bf16[6,512,128]{1,2,0:T(8,128)(2,1)}, u32[]{:S(2)}) copy-start(bf16[6,512,128]{1,2,0:T(8,128)(2,1)} %get-tuple-element.33) | copy-start | bytes 2359300
  395.3 55.6 %all-to-all-start.3 = ((bf16[6,2048,128]{2,0,1:T(8,128)(2,1)}), bf16[6,2048,128]{2,0,1:T(8,128)(2,1)}, u32[]{:S(2)}, u32[]{:S(2)}) async-start(bf16[6,2048,128]{2,0,1:T(8,128)(2,1)} %copy.76), calls=%async_computation.3 | async-start | bytes 8388608 | tf_op jit(solution)/shard_map/all_to_all | solution.py:69
  510.6 100.2 %all-to-all-start.6 = ((bf16[1,4,512,2048]{3,2,0,1:T(8,128)(2,1)}), bf16[1,4,512,2048]{3,2,0,1:T(8,128)(2,1)}, u32[]{:S(2)}, u32[]{:S(2)}) async-start(bf16[1,4,512,2048]{3,2,0,1:T(8,128)(2,1)} %maximum_bitcast_fusion), calls=%async_computation.6 | async-start | bytes 16777216 | tf_op jit(solution)/shard_map/all_to_all | solution.py:161
  635.4 30.3 %all-to-all-start.7 = ((bf16[2,512,512]{1,0,2:T(2,128)(2,1)}), bf16[2,512,512]{1,0,2:T(2,128)(2,1)S(1)}, u32[]{:S(2)}, u32[]{:S(2)}) async-start(bf16[2,512,512]{1,0,2:T(2,128)(2,1)} %copy.87), calls=%async_computation.7 | async-start | bytes 2097152 | tf_op jit(solution)/shard_map/all_to_all | solution.py:46
  661.2 8.0 %copy-start.3 = (f32[512,128]{1,0:T(8,128)S(1)}, f32[512,128]{1,0:T(8,128)}, u32[]{:S(2)}) copy-start(f32[512,128]{1,0:T(8,128)} %get-tuple-element.5) | copy-start | bytes 786436
  665.7 20.7 %all-to-all-start.8 = ((bf16[2,512,512]{1,0,2:T(2,128)(2,1)}), bf16[2,512,512]{1,0,2:T(2,128)(2,1)S(1)}, u32[]{:S(2)}, u32[]{:S(2)}) async-start(bf16[2,512,512]{1,0,2:T(2,128)(2,1)} %copy.90), calls=%async_computation.8 | async-start | bytes 2097152 | tf_op jit(solution)/shard_map/all_to_all | solution.py:45
  669.2 96.3 %all-reduce.2.cloned.1.call-start = ((), (), s32[]{:S(2)}) async-start(), calls=%async_computation.9 | async-start | bytes 1048576 | tf_op jit(solution)/shard_map/psum | solution.py:170
Sparse Core Ops, SparseCore 0:
  735.9 29.5 all-reduce.1
where the time goes:
time: 784 us; the launch traced here: 775 us
  matrix products  448 us (57%)
  waiting for transfers between devices  123 us (16%)
  other arithmetic  61.5 us (8%)
  local copies, waits for them, and re-layouts  54.4 us (7%)
  starting transfers between devices  40.7 us (5%)
  blocking collectives  32.9 us (4%)
  between operations  14.3 us (2%)
    all_to_all x1, waiting for transfers between devices, body(): lax.all_to_all(products[None], 'field', split_axis=1, concat_axis=0, tile...  93.2 us
    dot_general x2, matrix products, inverse(): jnp.dot(flat_im, isin.T, preferred_element_type=jnp.float32)  46.6 us
    dot_general x2, matrix products, inverse(): jnp.dot(flat_re, icos.T, preferred_element_type=jnp.float32)  44 us
    dot_general x2, matrix products, column_part(): jnp.dot(flat, cos_t, preferred_element_type=jnp.float32)  41 us
    dot_general x2, matrix products, inverse(): jnp.einsum('yk,mkj->myj', isin, z_re, preferred_element_type=jnp.float32)  40.5 us
    dot_general x2, matrix products, column_part(): jnp.dot(flat, sin_t, preferred_element_type=jnp.float32)  38.1 us
    dot_general x2, matrix products, inverse(): jnp.einsum('yk,mkj->myj', isin, z_im, preferred_element_type=jnp.float32)  37.2 us
    dot_general x2, matrix products, inverse(): jnp.einsum('yk,mkj->myj', icos, z_re, preferred_element_type=jnp.float32)  36.1 us
  transfers between devices with their start and end apart: 10, of which 2 were waited for; matrix products, arithmetic and copies ran while one was open for 38% of the time, Pallas kernels for 0%

commit v1 on v0

--- a/solution.py
+++ b/solution.py
@@ -5,6 +5,20 @@
 from jax.sharding import PartitionSpec as P
 
 TILE = 128
+
+
+def convert_block_on(chunk, in_dim, message):
+    r_now, s_next = (chunk.shape[:in_dim], chunk.shape[in_dim + 1 :])
+    v_next = chunk.reshape(*r_now, message, -1, *s_next)
+    response = jnp.moveaxis(v_next, in_dim, 0)
+    return response
+
+
+def enter_circles_now(point, pos_dim):
+    outer = list(point.shape[1:])
+    outer[pos_dim] *= point.shape[0]
+    z1 = jnp.moveaxis(point, 0, pos_dim).reshape(outer)
+    return z1
 
 
 def tables(npix, kf, scale):
@@ -64,9 +78,27 @@
         jnp.einsum("yk,mkj->myj", icos, z_im, preferred_element_type=jnp.float32)
         + jnp.einsum("yk,mkj->myj", isin, z_re, preferred_element_type=jnp.float32)
     ).astype(jnp.bfloat16)
+
+    def _launch_loops(raw, lane_axis, m, base_x):
+        known = lax.axis_size(lane_axis)
+        block_next = lax.axis_index(lane_axis)
+        far_arr, high = (known, block_next)
+        odd = convert_block_on(raw, m, far_arr)
+        table = [odd[high]]
+        for tick in range(1, far_arr):
+            out_arr = odd[high ^ tick]
+            block_now = lax.ppermute(
+                out_arr, lane_axis, [(hop_no, hop_no ^ tick) for hop_no in range(far_arr)]
+            )
+            table.append(block_now)
+        outcome_arr = jnp.stack(table)
+        odd = outcome_arr[high ^ jnp.arange(far_arr)]
+        near = enter_circles_now(odd, base_x)
+        return near
+
     y_re, y_im = (
         lax.all_to_all(y_re, "rows", split_axis=1, concat_axis=2, tiled=True),
-        lax.all_to_all(y_im, "rows", split_axis=1, concat_axis=2, tiled=True),
+        _launch_loops(y_im, "rows", 1, 2),
     )
     height = y_re.shape[1]
     flat_re = y_re.reshape(count * height, -1)

time: 784 us -> 824 us (1.051)
  local copies, waits for them, and re-layouts: 54.4 us -> 97.5 us
    unnamed x35 -> x63, local copies, waits for them, and re-layouts: 3.42 us -> 22.2 us
    another operation x0 -> x2, local copies, waits for them, and re-layouts: none -> 14.9 us
    convert_element_type x2 -> x0, local copies, waits for them, and re-layouts: 10.5 us -> none  [inverse(): y_im = (jnp.einsum('yk,mkj->myj', icos, z_im, preferred_element_type=jnp....]
    all_to_all x2 -> x0, starting transfers between devices: 9.3 us -> none  [inverse(): lax.all_to_all(y_im, 'rows', split_axis=1, concat_axis=2, tiled=True)]
    reshape x0 -> x2, local copies, waits for them, and re-layouts: none -> 8.67 us  [convert_block_on(): v_next = chunk.reshape(*r_now, message, -1, *s_next)]
  transfers between devices with their start and end apart: 10 -> 14, of which waited for: 2 -> 3; matrix products, arithmetic and copies ran while one was open for 38% -> 30% of each run, Pallas kernels for 0% -> 0%
where the time goes in v1:
time: 824 us; the launch traced here: 815 us
  matrix products  442 us (54%)
  waiting for transfers between devices  123 us (15%)
  local copies, waits for them, and re-layouts  97.5 us (12%)
  other arithmetic  64.7 us (8%)
  starting transfers between devices  36.6 us (4%)
  blocking collectives  35.4 us (4%)
  between operations  14.7 us (2%)
    all_to_all x1, waiting for transfers between devices, body(): lax.all_to_all(products[None], 'field', split_axis=1, concat_axis=0, tile...  93.2 us
    dot_general x2, matrix products, inverse(): jnp.dot(flat_im, isin.T, preferred_element_type=jnp.float32)  44.5 us
    dot_general x2, matrix products, inverse(): jnp.dot(flat_re, icos.T, preferred_element_type=jnp.float32)  41.2 us
    dot_general x2, matrix products, column_part(): jnp.dot(flat, cos_t, preferred_element_type=jnp.float32)  41 us
    dot_general x2, matrix products, inverse(): jnp.einsum('yk,mkj->myj', isin, z_re, preferred_element_type=jnp.float32)  40.5 us
    dot_general x2, matrix products, column_part(): jnp.dot(flat, sin_t, preferred_element_type=jnp.float32)  37.9 us
    dot_general x2, matrix products, inverse(): jnp.einsum('yk,mkj->myj', isin, z_im, preferred_element_type=jnp.float32)  37.9 us
    dot_general x2, matrix products, inverse(): jnp.einsum('yk,mkj->myj', icos, z_re, preferred_element_type=jnp.float32)  35.7 us
  transfers between devices with their start and end apart: 14, of which 3 were waited for; matrix products, arithmetic and copies ran while one was open for 30% of the time, Pallas kernels for 0%

profile of v1, /device:TPU:0, one launch (start us, length us, event | category | flops | bytes accessed | tf_op | source)
XLA Modules:
  0.0 814.7 jit_solution(5742021586027879278)
XLA Ops:
  10.6 16.8 %negate_convert_fusion.1 = bf16[1024,512]{1,0:T(8,128)(2,1)S(1)} fusion(bf16[1024,2048]{1,0:T(8,128)(2,1)S(1)} %bitcast.302, s32[512]{0:T(512)S(1)} %iota_add_fusion), kind=kOutput, calls=%fused_computation.87 | convolution fusion | flops 2165309440 | bytes 5244928 | tf_op jit(solution)/shard_map/dot_general | solution.py:50
  29.5 4.4 all-to-all-start.1
  34.0 18.9 %fusion.65 = bf16[1024,512]{1,0:T(8,128)(2,1)S(1)} fusion(bf16[1024,2048]{1,0:T(8,128)(2,1)} %bitcast.303, s32[512]{0:T(512)S(1)} %iota_add_fusion), kind=kOutput, calls=%fused_computation.98 | convolution fusion | flops 2164785152 | bytes 5244928 | tf_op jit(solution)/shard_map/dot_general | solution.py:45
  55.8 16.3 %select_reduce_fusion.2 = (f32[512,128]{1,0:T(8,128)}, f32[512,128]{1,0:T(8,128)S(1)}, f32[512,128]{1,0:T(8,128)S(1)}) fusion(f32[64]{0:T(128)S(1)} %copy-done.22, s32[512,128]{1,0:T(8,128)S(1)} %copy-done.12, f32[64]{0:T(128)S(1)} %get-tuple-element.12, f32[64]{0:T(128)S(1)} %get-tuple-element.13), kind=kLoop, calls=%fused_computation.5 | loop fusion | flops 29163520 | bytes 1049344 | tf_op jit(solution)/shard_map/reduce_sum | solution.py:130
  72.1 3.7 all-to-all-start
  80.9 15.9 %fusion.46 = f32[2,128,512]{2,1,0:T(8,128)S(1)} fusion(bf16[2,2048,128]{1,2,0:T(8,128)(2,1)S(1)} %all_to_all.88, s32[512]{0:T(512)S(1)} %iota_add_fusion), kind=kOutput, calls=%fused_computation.77 | convolution fusion | flops 553648128 | bytes 1574912 | tf_op jit(solution)/shard_map/yk,myj->mkj/dot_general | solution.py:62
  98.5 16.3 %fusion.44 = f32[2,128,512]{2,1,0:T(8,128)S(1)} fusion(bf16[2,2048,128]{1,2,0:T(8,128)(2,1)S(1)} %all_to_all.84, s32[512]{0:T(512)S(1)} %iota_add_fusion), kind=kOutput, calls=%fused_computation.75 | convolution fusion | flops 553648128 | bytes 1574912 | tf_op jit(solution)/shard_map/yk,myj->mkj/dot_general | solution.py:65
  114.9 16.0 %fusion.69 = f32[2,512,128]{1,2,0:T(8,128)S(1)} fusion(f32[2,128,512]{2,1,0:T(8,128)S(1)} %fusion.46, bf16[2,2048,128]{1,2,0:T(8,128)(2,1)S(1)} %all_to_all.84, s32[512]{0:T(512)S(1)} %iota_add_fusion), kind=kOutput, calls=%fused_computation.100 | convolution fusion | flops 553779200 | bytes 2099200 | tf_op jit(solution)/shard_map/yk,myj->mkj/dot_general | solution.py:62
  130.9 16.1 %fusion.75 = f32[2,512,128]{1,2,0:T(8,128)S(1)} fusion(f32[2,128,512]{2,1,0:T(8,128)S(1)} %fusion.44, bf16[2,2048,128]{1,2,0:T(8,128)(2,1)S(1)} %copy-done.11, s32[512]{0:T(512)S(1)} %iota_add_fusion), kind=kOutput, calls=%fused_computation.102 | convolution fusion | flops 553779200 | bytes 2099200 | tf_op jit(solution)/shard_map/yk,myj->mkj/dot_general | solution.py:65
  148.2 19.5 %fusion.38 = f32[6,128,2048]{2,1,0:T(8,128)} fusion(bf16[6,512,128]{1,2,0:T(8,128)(2,1)S(1)} %get-tuple-element.41, s32[512]{0:T(512)S(1)} %iota_add_fusion), kind=kOutput, calls=%fused_computation.69 | convolution fusion | flops 1627389952 | bytes 7079936 | tf_op jit(solution)/shard_map/yk,mkj->myj/dot_general | solution.py:74
  167.9 16.7 %fusion.36 = f32[6,128,2048]{2,1,0:T(8,128)S(1)} fusion(bf16[6,512,128]{1,2,0:T(8,128)(2,1)S(1)} %fusion.125, s32[512]{0:T(512)S(1)} %iota_add_fusion), kind=kOutput, calls=%fused_computation.67 | convolution fusion | flops 1627389952 | bytes 7079936 | tf_op jit(solution)/shard_map/yk,mkj->myj/dot_general | solution.py:78
  184.6 22.0 %fusion.21 = bf16[6,2048,128]{1,2,0:T(8,128)(2,1)} fusion(f32[6,128,2048]{2,1,0:T(8,128)S(1)} %fusion.36, bf16[6,512,128]{1,2,0:T(8,128)(2,1)S(1)} %get-tuple-element.41, s32[512]{0:T(512)S(1)} %iota_add_fusion), kind=kOutput, calls=%fused_computation.51 | convolution fusion | flops 1630535680 | bytes 10225664 | tf_op jit(solution)/shard_map/yk,mkj->myj/dot_general | solution.py:79
  206.6 4.8 reshape.564
  213.0 19.0 %all_gather.6 = bf16[4,512,128]{2,1,0:T(8,128)(2,1)} all-gather(bf16[1,512,128]{2,1,0:T(8,128)(2,1)} %copy.101), channel_id=1, replica_groups=mesh['real'=4,'rows'=4,'field'=2] {'real'}, dimensions={0}, use_global_device_ids=true | all-gather | bytes 655360 | tf_op jit(solution)/shard_map/all_gather | solution.py:172
  232.8 16.4 %all_gather.7 = bf16[4,512,128]{2,1,0:T(8,128)(2,1)S(1)} all-gather(bf16[1,512,128]{2,1,0:T(8,128)(2,1)} %copy.103), channel_id=1, replica_groups=mesh['real'=4,'rows'=4,'field'=2] {'real'}, dimensions={0}, use_global_device_ids=true | all-gather | bytes 655360 | tf_op jit(solution)/shard_map/all_gather | solution.py:178
  256.2 16.2 %fusion.34 = f32[3,128,2048]{2,1,0:T(8,128)S(1)} fusion(s32[512]{0:T(512)S(1)} %iota_add_fusion, bf16[1,512,128]{1,2,0:T(8,128)(2,1)S(1)} %get-tuple-element.33, bf16[1,512,128]{1,2,0:T(8,128)(2,1)S(1)} %get-tuple-element.32, bf16[1,512,128]{1,2,0:T(8,128)(2,1)S(1)} %get-tuple-element.44), kind=kOutput, calls=%fused_computation.65 | convolution fusion | flops 822476800 | bytes 3540992 | tf_op jit(solution)/shard_map/yk,mkj->myj/dot_general | solution.py:74
  272.4 17.3 %fusion.32 = f32[3,128,2048]{2,1,0:T(8,128)} fusion(s32[512]{0:T(512)S(1)} %iota_add_fusion, bf16[1,512,128]{1,2,0:T(8,128)(2,1)S(1)} %get-tuple-element.42, bf16[1,512,128]{1,2,0:T(8,128)(2,1)S(1)} %get-tuple-element.43, bf16[1,512,128]{1,2,0:T(8,128)(2,1)S(1)} %get-tuple-element.45), kind=kOutput, calls=%fused_computation.63 | convolution fusion | flops 822476800 | bytes 3540992 | tf_op jit(solution)/shard_map/yk,mkj->myj/dot_general | solution.py:78
  289.8 17.4 %fusion.22 = bf16[3,2048,128]{1,2,0:T(8,128)(2,1)} fusion(f32[3,128,2048]{2,1,0:T(8,128)S(1)} %fusion.34, s32[512]{0:T(512)S(1)} %iota_add_fusion, bf16[1,512,128]{1,2,0:T(8,128)(2,1)S(1)} %get-tuple-element.42, bf16[1,512,128]{1,2,0:T(8,128)(2,1)S(1)} %get-tuple-element.43, bf16[1,512,128]{1,2,0:T(8,128)(2,1)S(1)} %get-tuple-element.45), kind=kOutput, calls=%fused_computation.53 | convolution fusion | flops 824049664 | bytes 5113856 | tf_op jit(solution)/shard_map/yk,mkj->myj/dot_general | solution.py:75
  307.2 4.2 copy.105
  311.4 4.8 all-to-all-start.3
  316.2 18.6 %fusion.23 = bf16[3,2048,128]{1,2,0:T(8,128)(2,1)} fusion(f32[3,128,2048]{2,1,0:T(8,128)} %fusion.32, s32[512]{0:T(512)S(1)} %iota_add_fusion, bf16[1,512,128]{1,2,0:T(8,128)(2,1)S(1)} %copy-done.14, bf16[1,512,128]{1,2,0:T(8,128)(2,1)S(1)} %get-tuple-element.32, bf16[1,512,128]{1,2,0:T(8,128)(2,1)S(1)} %copy-done.16), kind=kOutput, calls=%fused_computation.54 | convolution fusion | flops 824049664 | bytes 5113856 | tf_op jit(solution)/shard_map/yk,mkj->myj/dot_general | solution.py:79
  334.8 3.9 reshape.566
  338.7 7.2 constant_dynamic-slice_fusion.3
  350.5 7.8 constant_dynamic-slice_fusion.7
  358.3 4.8 copy.124
  363.1 4.7 copy.123
  376.1 20.5 %fusion.20 = bf16[6,2048,128]{1,2,0:T(8,128)(2,1)} fusion(f32[6,128,2048]{2,1,0:T(8,128)} %fusion.38, bf16[6,512,128]{1,2,0:T(8,128)(2,1)} %copy-done.19, s32[512]{0:T(512)S(1)} %iota_add_fusion), kind=kOutput, calls=%fused_computation.50 | convolution fusion | flops 1630535680 | bytes 10225664 | tf_op jit(solution)/shard_map/yk,mkj->myj/dot_general | solution.py:75
  396.6 6.5 copy.94
  412.8 4.9 all-to-all-start.2
  422.6 4.3 copy.100
  430.0 17.3 %fusion.60 = f32[1536,2048]{1,0:T(8,128)S(1)} fusion(s32[512]{0:T(512)S(1)} %iota_add_fusion, bf16[192,8,4,128]{3,2,1,0:T(4,128)(2,1)S(1)} %bitcast.317), kind=kOutput, calls=%fused_computation.92 | convolution fusion | flops 3238002688 | bytes 14157824 | tf_op jit(solution)/shard_map/dot_general | solution.py:106
  447.3 20.8 %fusion = f32[1536,2048]{1,0:T(8,128)} fusion(f32[1536,2048]{1,0:T(8,128)S(1)} %fusion.60, s32[512]{0:T(512)S(1)} %iota_add_fusion, bf16[192,8,4,128]{3,2,1,0:T(4,128)(2,1)S(1)} %bitcast.318), kind=kOutput, calls=%fused_computation.9 | convolution fusion | flops 3247439872 | bytes 26740736 | tf_op jit(solution)/shard_map/dot_general | solution.py:106
  468.1 4.6 copy.95
  472.7 23.9 %fusion.17 = f32[3072,2048]{1,0:T(8,128)} fusion(bf16[384,8,4,128]{3,2,1,0:T(4,128)(2,1)S(1)} %bitcast.311, s32[512]{0:T(512)S(1)} %iota_add_fusion), kind=kOutput, calls=%fused_computation.44 | convolution fusion | flops 6459228160 | bytes 28313600 | tf_op jit(solution)/shard_map/dot_general | solution.py:106
  496.6 23.7 %subtract_convert_fusion = bf16[3072,2048]{1,0:T(8,128)(2,1)S(1)} fusion(f32[3072,2048]{1,0:T(8,128)} %fusion.17, bf16[384,8,4,128]{3,2,1,0:T(4,128)(2,1)S(1)} %bitcast.312, s32[512]{0:T(512)S(1)} %iota_add_fusion), kind=kOutput, calls=%fused_computation.2 | convolution fusion | flops 6471811072 | bytes 40896512 | tf_op jit(solution)/shard_map/dot_general | solution.py:106
  520.4 9.3 %slice_convert_fusion.1 = (f32[1536,2048]{1,0:T(8,128)}, f32[1536,2048]{1,0:T(8,128)}) fusion(bf16[3072,2048]{1,0:T(8,128)(2,1)S(1)} %subtract_convert_fusion), kind=kLoop, calls=%fused_computation.11 | loop fusion | flops 6291456 | bytes 37748736 | tf_op jit(solution)/shard_map/convert_element_type | solution.py:165
  529.7 15.9 %fusion.24 = (bf16[1,1,512,2048]{3,2,1,0:T(8,128)(2,1)S(1)}, bf16[1,1,512,2048]{3,2,1,0:T(8,128)(2,1)S(1)}, bf16[1,1,512,2048]{3,2,1,0:T(8,128)(2,1)S(1)}, bf16[1,1,512,2048]{3,2,1,0:T(8,128)(2,1)}) fusion(f32[1536,2048]{1,0:T(8,128)} %get-tuple-element.20, f32[1536,2048]{1,0:T(8,128)} %get-tuple-element.21, f32[1536,2048]{1,0:T(8,128)} %fusion), kind=kLoop, calls=%fused_computation.55 | loop fusion | flops 16777216 | bytes 46137344 | tf_op jit(solution)/shard_map/stack | solution.py:191
  545.6 5.7 maximum_bitcast_fusion
  551.3 7.0 all-to-all-start.4
  558.3 93.2 %all-to-all-done.4 = bf16[1,4,512,2048]{3,2,0,1:T(8,128)(2,1)} async-done(((bf16[1,4,512,2048]{3,2,0,1:T(8,128)(2,1)}), bf16[1,4,512,2048]{3,2,0,1:T(8,128)(2,1)}, u32[]{:S(2)}, u32[]{:S(2)}) %all-to-all-start.4) | async-done | bytes 8388640 | tf_op jit(solution)/shard_map/all_to_all | solution.py:193
  651.5 21.1 %negate_convert_fusion = bf16[2048,512]{1,0:T(8,128)(2,1)S(1)} fusion(bf16[2048,2048]{1,0:T(8,128)(2,1)} %bitcast.50, s32[512]{0:T(512)S(1)} %iota_add_fusion), kind=kOutput, calls=%fused_computation.33 | convolution fusion | flops 4313841664 | bytes 10487808 | tf_op jit(solution)/shard_map/dot_general | solution.py:50
  675.8 3.9 all-to-all-start.5
  679.8 22.1 %convolution_convert_fusion = bf16[2048,512]{1,0:T(8,128)(2,1)} fusion(bf16[2048,2048]{1,0:T(8,128)(2,1)} %bitcast.50, s32[512]{0:T(512)S(1)} %iota_add_fusion), kind=kOutput, calls=%fused_computation.52 | convolution fusion | flops 4312793088 | bytes 10487808 | tf_op jit(solution)/shard_map/dot_general | solution.py:45
  710.7 16.8 %fusion.40 = f32[2,128,512]{2,1,0:T(8,128)} fusion(bf16[2,2048,128]{1,2,0:T(8,128)(2,1)S(1)} %bitcast.320, s32[512]{0:T(512)S(1)} %iota_add_fusion), kind=kOutput, calls=%fused_computation.71 | convolution fusion | flops 553648128 | bytes 1574912 | tf_op jit(solution)/shard_map/yk,myj->mkj/dot_general | solution.py:62
  727.8 16.1 %fusion.42 = f32[2,128,512]{2,1,0:T(8,128)S(1)} fusion(bf16[2,2048,128]{1,2,0:T(8,128)(2,1)S(1)} %bitcast.322, s32[512]{0:T(512)S(1)} %iota_add_fusion), kind=kOutput, calls=%fused_computation.73 | convolution fusion | flops 553648128 | bytes 1574912 | tf_op jit(solution)/shard_map/yk,myj->mkj/dot_general | solution.py:65
  744.0 16.1 %fusion.102 = bf16[2,1,512,128]{2,3,0,1:T(8,128)(2,1)S(1)} fusion(f32[2,128,512]{2,1,0:T(8,128)S(1)} %copy-done.26, bf16[2,2048,128]{1,2,0:T(8,128)(2,1)S(1)} %bitcast.323, s32[512]{0:T(512)S(1)} %iota_add_fusion, f32[512,128]{0,1:T(8,128)S(1)} %copy.119), kind=kOutput, calls=%fused_computation.111 | convolution fusion | flops 554041344 | bytes 2099200 | tf_op jit(solution)/shard_map/yk,myj->mkj/dot_general | solution.py:62
  760.1 16.1 %fusion.105 = bf16[2,1,512,128]{2,3,0,1:T(8,128)(2,1)S(1)} fusion(f32[2,128,512]{2,1,0:T(8,128)S(1)} %fusion.42, bf16[2,2048,128]{1,2,0:T(8,128)(2,1)S(1)} %bitcast.321, s32[512]{0:T(512)S(1)} %iota_add_fusion, f32[512,128]{0,1:T(8,128)S(1)} %copy.87), kind=kOutput, calls=%fused_computation.112 | convolution fusion | flops 554041344 | bytes 2099200 | tf_op jit(solution)/shard_map/yk,myj->mkj/dot_general | solution.py:65
  777.1 28.0 %all-reduce.2.cloned.1.call-done = bf16[1,2,2,512,128]{3,4,1,2,0:T(8,128)(2,1)} async-done(((bf16[1,2,2,512,128]{3,4,1,2,0:T(8,128)(2,1)}), bf16[1,2,2,512,128]{3,4,1,2,0:T(8,128)(2,1)}) %all-reduce.2.cloned.1.call-update) | async-done | bytes 524304 | tf_op jit(solution)/shard_map/psum | solution.py:202
  (134 shorter events, 72.3 us)
Async XLA Ops:
  6.5 1.8 copy-start.7
  10.6 16.8 %copy-start.3 = (bf16[2,512,2048]{2,1,0:T(8,128)(2,1)}, bf16[2,512,2048]{2,1,0:T(8,128)(2,1)S(1)}, u32[]{:S(2)}) copy-start(bf16[2,512,2048]{2,1,0:T(8,128)(2,1)S(1)} %maximum_select_fusion) | copy-start | bytes 12582916
  29.5 42.5 %all-to-all-start.1 = ((bf16[2,512,512]{1,0,2:T(2,128)(2,1)}), bf16[2,512,512]{1,0,2:T(2,128)(2,1)S(1)}, u32[]{:S(2)}, u32[]{:S(2)}) async-start(bf16[2,512,512]{1,0,2:T(2,128)(2,1)} %copy.91), calls=%async_computation.1 | async-start | bytes 2097152 | tf_op jit(solution)/shard_map/all_to_all | solution.py:60
  33.9 21.1 %copy-start.23 = (f32[1,64]{1,0:T(1,128)S(1)}, f32[1,64]{1,0:T(1,128)}, u32[]{:S(2)}) copy-start(f32[1,64]{1,0:T(1,128)} %param.12) | copy-start | bytes 772
  33.9 21.1 %copy-start.24 = (f32[1,64]{1,0:T(1,128)S(1)}, f32[1,64]{1,0:T(1,128)}, u32[]{:S(2)}) copy-start(f32[1,64]{1,0:T(1,128)} %param.13) | copy-start | bytes 772
  34.0 21.1 %copy-start.25 = (s32[4]{0:T(128)S(1)}, s32[4]{0:T(128)}, u32[]{:S(2)}) copy-start(s32[4]{0:T(128)} %param.15) | copy-start | bytes 52
  34.0 21.8 %copy-start.12 = (s32[512,128]{1,0:T(8,128)S(1)}, s32[512,128]{1,0:T(8,128)}, u32[]{:S(2)}) copy-start(s32[512,128]{1,0:T(8,128)} %param.11) | copy-start | bytes 786436
  34.0 21.8 %copy-start.22 = (f32[64]{0:T(128)S(1)}, f32[64]{0:T(128)}, u32[]{:S(2)}) copy-start(f32[64]{0:T(128)} %param.14) | copy-start | bytes 772
  52.9 202.1 %copy-start.17 = (f32[512]{0:T(512)}, f32[512]{0:T(512)S(1)}, u32[]{:S(2)}) copy-start(f32[512]{0:T(512)S(1)} %convert_multiply_fusion) | copy-start | bytes 6148
  55.0 200.0 %copy-start.20 = (f32[128]{0:T(128)}, f32[128]{0:T(128)S(1)}, u32[]{:S(2)}) copy-start(f32[128]{0:T(128)S(1)} %convert_multiply_fusion.1) | copy-start | bytes 1540
  72.1 24.8 %all-to-all-start = ((bf16[2,512,512]{1,0,2:T(2,128)(2,1)}), bf16[2,512,512]{1,0,2:T(2,128)(2,1)S(1)}, u32[]{:S(2)}, u32[]{:S(2)}) async-start(bf16[2,512,512]{1,0,2:T(2,128)(2,1)} %copy.89), calls=%async_computation | async-start | bytes 2097152 | tf_op jit(solution)/shard_map/all_to_all | solution.py:59
  77.1 70.9 %copy-start = (f32[512,128]{0,1:T(8,128)}, f32[512,128]{0,1:T(8,128)S(1)}, u32[]{:S(2)}) copy-start(f32[512,128]{0,1:T(8,128)S(1)} %copy.88) | copy-start | bytes 786436
  80.9 16.0 %copy-start.10 = (bf16[2,2048,128]{1,2,0:T(8,128)(2,1)}, bf16[2,2048,128]{1,2,0:T(8,128)(2,1)S(1)}, u32[]{:S(2)}) copy-start(bf16[2,2048,128]{1,2,0:T(8,128)(2,1)S(1)} %all_to_all.88) | copy-start | bytes 3145732
  114.9 16.0 %copy-start.11 = (bf16[2,2048,128]{1,2,0:T(8,128)(2,1)S(1)}, bf16[2,2048,128]{1,2,0:T(8,128)(2,1)}, u32[]{:S(2)}) copy-start(bf16[2,2048,128]{1,2,0:T(8,128)(2,1)} %copy-done.10) | copy-start | bytes 3145732
  167.8 16.7 %copy-start.19 = (bf16[6,512,128]{1,2,0:T(8,128)(2,1)}, bf16[6,512,128]{1,2,0:T(8,128)(2,1)S(1)}, u32[]{:S(2)}) copy-start(bf16[6,512,128]{1,2,0:T(8,128)(2,1)S(1)} %fusion.125) | copy-start | bytes 2359300
  256.2 16.2 %copy-start.13 = (bf16[1,512,128]{1,2,0:T(8,128)(2,1)}, bf16[1,512,128]{1,2,0:T(8,128)(2,1)S(1)}, u32[]{:S(2)}) copy-start(bf16[1,512,128]{1,2,0:T(8,128)(2,1)S(1)} %get-tuple-element.33) | copy-start | bytes 393220
  256.2 16.2 %copy-start.15 = (bf16[1,512,128]{1,2,0:T(8,128)(2,1)}, bf16[1,512,128]{1,2,0:T(8,128)(2,1)S(1)}, u32[]{:S(2)}) copy-start(bf16[1,512,128]{1,2,0:T(8,128)(2,1)S(1)} %get-tuple-element.44) | copy-start | bytes 393220
  307.2 9.0 %copy-start.14 = (bf16[1,512,128]{1,2,0:T(8,128)(2,1)S(1)}, bf16[1,512,128]{1,2,0:T(8,128)(2,1)}, u32[]{:S(2)}) copy-start(bf16[1,512,128]{1,2,0:T(8,128)(2,1)} %copy-done.13) | copy-start | bytes 393220
  307.2 9.0 %copy-start.16 = (bf16[1,512,128]{1,2,0:T(8,128)(2,1)S(1)}, bf16[1,512,128]{1,2,0:T(8,128)(2,1)}, u32[]{:S(2)}) copy-start(bf16[1,512,128]{1,2,0:T(8,128)(2,1)} %copy-done.15) | copy-start | bytes 393220
  311.4 101.5 %all-to-all-start.3 = ((bf16[3,2048,128]{2,0,1:T(4,128)(2,1)}), bf16[3,2048,128]{2,0,1:T(4,128)(2,1)}, u32[]{:S(2)}, u32[]{:S(2)}) async-start(bf16[3,2048,128]{2,0,1:T(4,128)(2,1)} %copy.105), calls=%async_computation.3 | async-start | bytes 4194304 | tf_op jit(solution)/shard_map/all_to_all | solution.py:100
  348.7 27.1 %collective-permute-start.5 = (bf16[3,512,128]{2,1,0:T(8,128)(2,1)}, bf16[3,512,128]{2,1,0:T(8,128)(2,1)}, u32[]{:S(2)}, u32[]{:S(2)}) collective-permute-start(bf16[3,512,128]{2,1,0:T(8,128)(2,1)} %bitcast.331), channel_id=1, source_target_pairs={{0,6},{2,4},{4,2},{6,0},{1,7},{3,5},{5,3},{7,1},{8,14},{10,12},{12... | collective-permute-start | bytes 1179656 | tf_op jit(solution)/shard_map/ppermute | solution.py:90
  358.2 11.5 %copy-start.2 = (bf16[6,1,512,128]{2,1,3,0:T(2,128)(2,1)S(1)}, bf16[6,1,512,128]{2,1,3,0:T(2,128)(2,1)}, u32[]{:S(2)}) copy-start(bf16[6,1,512,128]{2,1,3,0:T(2,128)(2,1)} %get-tuple-element.24) | copy-start | bytes 2359300
  358.2 14.1 %copy-start.6 = (bf16[3,1,512,128]{2,1,3,0:T(2,128)(2,1)S(1)}, bf16[3,1,512,128]{2,1,3,0:T(2,128)(2,1)}, u32[]{:S(2)}) copy-start(bf16[3,1,512,128]{2,1,3,0:T(2,128)(2,1)} %get-tuple-element.27) | copy-start | bytes 1179652
  358.2 16.0 %copy-start.5 = (bf16[3,1,512,128]{2,1,3,0:T(2,128)(2,1)S(1)}, bf16[3,1,512,128]{2,1,3,0:T(2,128)(2,1)}, u32[]{:S(2)}) copy-start(bf16[3,1,512,128]{2,1,3,0:T(2,128)(2,1)} %get-tuple-element.28) | copy-start | bytes 1179652
  363.1 54.7 %collective-permute-start.2 = (bf16[6,512,128]{2,1,0:T(8,128)(2,1)}, bf16[6,512,128]{2,1,0:T(8,128)(2,1)}, u32[]{:S(2)}, u32[]{:S(2)}) collective-permute-start(bf16[6,512,128]{2,1,0:T(8,128)(2,1)} %bitcast.326), channel_id=1, source_target_pairs={{0,6},{2,4},{4,2},{6,0},{1,7},{3,5},{5,3},{7,1},{8,14},{10,12},{12... | collective-permute-start | bytes 2359304 | tf_op jit(solution)/shard_map/ppermute | solution.py:90
  367.8 50.0 %collective-permute-start.1 = (bf16[6,512,128]{2,1,0:T(8,128)(2,1)}, bf16[6,512,128]{2,1,0:T(8,128)(2,1)}, u32[]{:S(2)}, u32[]{:S(2)}) collective-permute-start(bf16[6,512,128]{2,1,0:T(8,128)(2,1)} %bitcast.327), channel_id=1, source_target_pairs={{0,4},{2,6},{4,0},{6,2},{1,5},{3,7},{5,1},{7,3},{8,12},{10,14},{12... | collective-permute-start | bytes 2359304 | tf_op jit(solution)/shard_map/ppermute | solution.py:90
  372.4 45.4 %collective-permute-start = (bf16[6,512,128]{2,1,0:T(8,128)(2,1)}, bf16[6,512,128]{2,1,0:T(8,128)(2,1)}, u32[]{:S(2)}, u32[]{:S(2)}) collective-permute-start(bf16[6,512,128]{2,1,0:T(8,128)(2,1)} %bitcast.328), channel_id=1, source_target_pairs={{0,2},{2,0},{4,6},{6,4},{1,3},{3,1},{5,7},{7,5},{8,10},{10,8},{12,... | collective-permute-start | bytes 2359304 | tf_op jit(solution)/shard_map/ppermute | solution.py:90
  374.0 34.4 %collective-permute-start.4 = (bf16[3,512,128]{2,1,0:T(8,128)(2,1)}, bf16[3,512,128]{2,1,0:T(8,128)(2,1)S(1)}, u32[]{:S(2)}, u32[]{:S(2)}) collective-permute-start(bf16[3,512,128]{2,1,0:T(8,128)(2,1)} %bitcast.41), channel_id=1, source_target_pairs={{0,4},{2,6},{4,0},{6,2},{1,5},{3,7},{5,1},{7,3},{8,12},{10,14},{12... | collective-permute-start | bytes 1179656 | tf_op jit(solution)/shard_map/ppermute | solution.py:90
  375.8 32.6 %collective-permute-start.3 = (bf16[3,512,128]{2,1,0:T(8,128)(2,1)}, bf16[3,512,128]{2,1,0:T(8,128)(2,1)S(1)}, u32[]{:S(2)}, u32[]{:S(2)}) collective-permute-start(bf16[3,512,128]{2,1,0:T(8,128)(2,1)} %bitcast.39), channel_id=1, source_target_pairs={{0,2},{2,0},{4,6},{6,4},{1,3},{3,1},{5,7},{7,5},{8,10},{10,8},{12,... | collective-permute-start | bytes 1179656 | tf_op jit(solution)/shard_map/ppermute | solution.py:90
  396.6 6.5 copy-start.1
  396.6 9.1 %copy-start.4 = (bf16[3,1,512,128]{2,1,3,0:T(2,128)(2,1)S(1)}, bf16[3,1,512,128]{2,1,3,0:T(2,128)(2,1)}, u32[]{:S(2)}) copy-start(bf16[3,1,512,128]{2,1,3,0:T(2,128)(2,1)} %get-tuple-element.26) | copy-start | bytes 1179652
  412.8 55.2 %all-to-all-start.2 = ((bf16[6,2048,128]{2,0,1:T(8,128)(2,1)}), bf16[6,2048,128]{2,0,1:T(8,128)(2,1)}, u32[]{:S(2)}, u32[]{:S(2)}) async-start(bf16[6,2048,128]{2,0,1:T(8,128)(2,1)} %copy.94), calls=%async_computation.2 | async-start | bytes 8388608 | tf_op jit(solution)/shard_map/all_to_all | solution.py:100
  430.0 17.3 %copy-start.8 = (bf16[3,512,4,128]{3,2,1,0:T(4,128)(2,1)S(1)}, bf16[3,512,4,128]{3,2,1,0:T(4,128)(2,1)}, u32[]{:S(2)}) copy-start(bf16[3,512,4,128]{3,2,1,0:T(4,128)(2,1)} %copy.111) | copy-start | bytes 4718596
  551.3 100.2 %all-to-all-start.4 = ((bf16[1,4,512,2048]{3,2,0,1:T(8,128)(2,1)}), bf16[1,4,512,2048]{3,2,0,1:T(8,128)(2,1)}, u32[]{:S(2)}, u32[]{:S(2)}) async-start(bf16[1,4,512,2048]{3,2,0,1:T(8,128)(2,1)} %maximum_bitcast_fusion), calls=%async_computation.4 | async-start | bytes 16777216 | tf_op jit(solution)/shard_map/all_to_all | solution.py:193
  675.8 30.5 %all-to-all-start.5 = ((bf16[2,512,512]{1,0,2:T(2,128)(2,1)}), bf16[2,512,512]{1,0,2:T(2,128)(2,1)S(1)}, u32[]{:S(2)}, u32[]{:S(2)}) async-start(bf16[2,512,512]{1,0,2:T(2,128)(2,1)} %copy.113), calls=%async_computation.5 | async-start | bytes 2097152 | tf_op jit(solution)/shard_map/all_to_all | solution.py:60
  701.9 8.1 copy-start.9
  701.9 8.1 copy-start.18
  701.9 8.1 copy-start.21
  706.4 21.1 %all-to-all-start.6 = ((bf16[2,512,512]{1,0,2:T(2,128)(2,1)}), bf16[2,512,512]{1,0,2:T(2,128)(2,1)S(1)}, u32[]{:S(2)}, u32[]{:S(2)}) async-start(bf16[2,512,512]{1,0,2:T(2,128)(2,1)} %copy.116), calls=%async_computation.6 | async-start | bytes 2097152 | tf_op jit(solution)/shard_map/all_to_all | solution.py:59
  709.9 95.2 %all-reduce.2.cloned.1.call-start = ((), (), s32[]{:S(2)}) async-start(), calls=%async_computation.7 | async-start | bytes 1048576 | tf_op jit(solution)/shard_map/psum | solution.py:202
  727.8 16.2 %copy-start.26 = (f32[2,128,512]{2,1,0:T(8,128)S(1)}, f32[2,128,512]{2,1,0:T(8,128)}, u32[]{:S(2)}) copy-start(f32[2,128,512]{2,1,0:T(8,128)} %fusion.40) | copy-start | bytes 1572868
Sparse Core Ops, SparseCore 0:
  777.2 27.8 all-reduce.1
